TPU v7x, 32 devices: a whole 2x2x4 slice. The times are simulated.
32 devices in a mesh: groups: 2 (over y), mem: 4 (over z), head: 2 (over x), width: 2 (over core).
Axes of the slice: x: 2, y: 2, z: 4, core: 2. Of those that a mesh axis runs over, the one named last changes fastest.
Arguments:
- residual_in: bfloat16 [64, 5120], P('groups', 'mem'), parts along dimension 0, may hold values from -26 to 26
- attention_gain: float32 [5120], P('mem'), may hold values from 0.5 to 1.5
- query_weight: bfloat16 [5120, 8192], P('mem', ('head', 'width')), may hold values from -0.078125 to 0.078125
- key_weight: bfloat16 [5120, 1024], P('mem', ('head', 'width')), may hold values from -0.078125 to 0.078125
- value_weight: bfloat16 [5120, 1024], P('mem', ('head', 'width')), may hold values from -0.078125 to 0.078125
- query_norm: float32 [128], replicated, may hold values from 0.25 to 1.75
- key_norm: float32 [128], replicated, may hold values from 0.1 to 1.9
- cache_keys: bfloat16 [65536, 8, 128], P(('groups', 'mem'), ('head', 'width')), parts along dimension 0, may hold values from -480 to 480
- cache_values: bfloat16 [65536, 8, 128], P(('groups', 'mem'), ('head', 'width')), parts along dimension 0, may hold values from -12 to 12
- slot_request: int32 [65536], P(('groups', 'mem')), parts along dimension 0, may hold values from 0 to 16, as said below
- lengths: int32 [32], P('groups'), parts along dimension 0, may hold values from 1056 to 1760, as said below
- output_weight: bfloat16 [8192, 5120], P(('head', 'width'), 'mem'), may hold values from -0.0625 to 0.0625
- second_gain: float32 [5120], P('mem'), may hold values from 0.5 to 1.5
- gate_weight: bfloat16 [5120, 25600], P('mem', ('head', 'width')), may hold values from -0.078125 to 0.078125
- up_weight: bfloat16 [5120, 25600], P('mem', ('head', 'width')), may hold values from -0.078125 to 0.078125
- down_weight: bfloat16 [25600, 5120], P(('head', 'width'), 'mem'), may hold values from -0.0390625 to 0.0390625
Outputs:
- layer_out: bfloat16 [64, 5120], P('groups', 'mem'), parts along dimension 0
There are 2 independent parts, one for each index of `groups`. A program takes and returns all parts, laid end to end along the dimension named above; an argument that names none is the same for every part. Nothing has to cross between parts.
Inputs may be any that keep to these rules, and one draw needn't show every extreme that they name: slot_request[s] names the request whose cached token sits in slot s, or is 16 for an empty slot. On each owner (each aligned block of 8192 slots along mem) the used slots come first; taking owners in order and their used slots in order, requests 0 to 15 follow one another in consecutive slots, so a request may continue on the next owner, but on no further one: a request's slots lie on at most two consecutive owners. Request r has exactly lengths[r] slots. Some owner has all its slots used. lengths[r] is the number of cached tokens of request r; its new tokens stand at positions lengths[r] and lengths[r] + 1.
All inputs are finite; a program needn't handle non-finite values.
Results may differ from a plain program's by a relative error of at most 0.0095.
The roundings to bfloat16 on the way count: a program that leaves them out, or rounds other values in their place, can miss the bound.
Values may be sent and summed in bfloat16 or wider, within the bound.
A program may use at most 128 MiB of HBM per device.

v0:
```python
import math
import jax
import jax.numpy as jnp
from jax import lax
from jax.sharding import PartitionSpec as P

D = 5120
epsilon = 1e-06
rope_base = 1000000.0
floor_score = -1e30


def combined_all(value, axis, join):
    pieces = jax.tree.map(lambda part: lax.all_gather(part, axis), value)
    head = jax.tree.map(lambda part: part[0], pieces)
    tail = jax.tree.map(lambda part: part[1:], pieces)
    running, _ = lax.scan(lambda running, slab: (join(running, slab), None), head, tail)
    return running


def rotate(values, places):
    breadth = values.shape[-1]
    halfway = breadth // 2
    frequency = rope_base ** (-(jnp.arange(halfway, dtype=jnp.float32) * 2.0) / breadth)
    angles = places[..., None] * frequency
    cosine = jnp.cos(angles)
    sine_part = jnp.sin(angles)
    leading = values[..., :halfway]
    trailing = values[..., halfway:]
    return jnp.concatenate(
        [leading * cosine - trailing * sine_part, trailing * cosine + leading * sine_part], axis=-1
    )


def head_norm(values, scaling):
    mean_square = jnp.mean(values * values, axis=-1, keepdims=True)
    return values * lax.rsqrt(mean_square + epsilon) * scaling


def combine(first, second):
    first_top, first_sum, first_acc = first
    second_top, second_sum, second_acc = second
    highest = jnp.maximum(first_top, second_top)
    first_factor = jnp.exp(first_top - highest)
    second_factor = jnp.exp(second_top - highest)
    return (
        highest,
        first_sum * first_factor + second_sum * second_factor,
        first_acc * first_factor[..., None] + second_acc * second_factor[..., None],
    )


def per_device(
    residual_in,
    attention_gain,
    query_weight,
    key_weight,
    value_weight,
    query_norm,
    key_norm,
    cache_keys,
    cache_values,
    slot_request,
    lengths,
    output_weight,
    second_gain,
    gate_weight,
    up_weight,
    down_weight,
):
    row_count = residual_in.shape[0]
    requests = row_count // 2
    head_dim = query_norm.shape[0]
    kv_here = cache_keys.shape[1]
    q_here = query_weight.shape[1] // head_dim
    group_size = q_here // kv_here
    score_scale = 1.0 / math.sqrt(head_dim)
    residual = residual_in.astype(jnp.float32)
    squares = lax.psum(jnp.sum(residual * residual, axis=1), "mem")
    normed = (residual * lax.rsqrt(squares / D + epsilon)[:, None] * attention_gain).astype(
        jnp.bfloat16
    )
    query_part = jnp.dot(normed, query_weight, preferred_element_type=jnp.float32)
    key_part = jnp.dot(normed, key_weight, preferred_element_type=jnp.float32)
    value_part = jnp.dot(normed, value_weight, preferred_element_type=jnp.float32)
    offsets = jnp.arange(2, dtype=jnp.int32)
    places = (lengths[:, None] + offsets[None, :]).reshape(row_count).astype(jnp.float32)
    query_sum, key_sum, value_sum = lax.psum((query_part, key_part, value_part), "mem")
    count_rows = query_sum.shape[0]
    query_rot = rotate(
        head_norm(query_sum.reshape(count_rows, q_here, head_dim), query_norm), places[:, None]
    )
    key_rot = rotate(
        head_norm(key_sum.reshape(count_rows, kv_here, head_dim), key_norm), places[:, None]
    )
    queries = query_rot.astype(jnp.bfloat16)
    new_keys = key_rot.astype(jnp.bfloat16)
    new_values = value_sum.reshape(count_rows, kv_here, head_dim).astype(jnp.bfloat16)
    queries_split = queries.reshape(row_count, kv_here, group_size, head_dim)
    row_owner = jnp.arange(row_count, dtype=jnp.int32) // 2
    capacity = cache_keys.shape[0]
    block_size = min(1024, capacity)
    used_slots = jnp.sum((slot_request < requests).astype(jnp.int32))
    used_blocks = (used_slots + block_size - 1) // block_size
    start_state = (
        jnp.full((row_count, kv_here, group_size), floor_score, jnp.float32),
        jnp.zeros((row_count, kv_here, group_size), jnp.float32),
        jnp.zeros((row_count, kv_here, group_size, head_dim), jnp.float32),
    )

    def visit_block(counter, carried):
        highest, summed, running = carried
        first_slot = counter * block_size
        key_block = lax.dynamic_slice_in_dim(cache_keys, first_slot, block_size, 0)
        value_block = lax.dynamic_slice_in_dim(cache_values, first_slot, block_size, 0)
        owner_block = lax.dynamic_slice_in_dim(slot_request, first_slot, block_size, 0)
        scores = (
            jnp.einsum(
                "bkgd,skd->bkgs", queries_split, key_block, preferred_element_type=jnp.float32
            )
            * score_scale
        )
        matches = (owner_block[None, :] == row_owner[:, None])[:, None, None, :]
        block_top = jnp.max(jnp.where(matches, scores, floor_score), axis=-1)
        updated = jnp.maximum(highest, block_top)
        weights = jnp.where(matches, jnp.exp(scores - updated[..., None]), 0.0)
        factor = jnp.exp(highest - updated)
        summed = summed * factor + jnp.sum(weights, axis=-1)
        running = running * factor[..., None] + jnp.einsum(
            "bkgs,skd->bkgd",
            weights.astype(jnp.bfloat16),
            value_block,
            preferred_element_type=jnp.float32,
        )
        return (updated, summed, running)

    highest, summed, running = lax.fori_loop(0, used_blocks, visit_block, start_state)
    highest, summed, running = combined_all((highest, summed, running), "mem", combine)
    query_pairs = queries.reshape(requests, 2, kv_here, group_size, head_dim)
    key_pairs = new_keys.reshape(requests, 2, kv_here, head_dim)
    value_pairs = new_values.reshape(requests, 2, kv_here, head_dim)
    allowed = (offsets[None, :] <= offsets[:, None])[None, :, None, None, :]
    allowed_rows = jnp.broadcast_to(allowed, (requests, 2, kv_here, group_size, 2)).reshape(
        row_count, kv_here, group_size, 2
    )
    own_scores = (
        jnp.einsum("rtkgd,rskd->rtkgs", query_pairs, key_pairs, preferred_element_type=jnp.float32)
        * score_scale
    )
    own_scores = jnp.where(allowed, own_scores, floor_score).reshape(
        row_count, kv_here, group_size, 2
    )
    final_top = jnp.maximum(highest, jnp.max(own_scores, axis=-1))
    own_weights = jnp.where(allowed_rows, jnp.exp(own_scores - final_top[..., None]), 0.0)
    factor = jnp.exp(highest - final_top)
    summed = summed * factor + jnp.sum(own_weights, axis=-1)
    own_rounded = own_weights.astype(jnp.bfloat16).reshape(requests, 2, kv_here, group_size, 2)
    own_values = jnp.einsum(
        "rtkgs,rskd->rtkgd", own_rounded, value_pairs, preferred_element_type=jnp.float32
    )
    running = running * factor[..., None] + own_values.reshape(
        row_count, kv_here, group_size, head_dim
    )
    attended = (
        (running / summed[..., None]).reshape(row_count, q_here * head_dim).astype(jnp.bfloat16)
    )
    projected = lax.psum(
        jnp.dot(attended, output_weight, preferred_element_type=jnp.float32), ("head", "width")
    )
    middle = (residual + projected).astype(jnp.bfloat16)
    middle_wide = middle.astype(jnp.float32)
    squares_mid = lax.psum(jnp.sum(middle_wide * middle_wide, axis=1), "mem")
    normed_mid = (middle_wide * lax.rsqrt(squares_mid / D + epsilon)[:, None] * second_gain).astype(
        jnp.bfloat16
    )
    gate_part = jnp.dot(normed_mid, gate_weight, preferred_element_type=jnp.float32)
    up_part = jnp.dot(normed_mid, up_weight, preferred_element_type=jnp.float32)
    gate_sum, up_sum = (
        lax.psum_scatter(gate_part, "mem", scatter_dimension=0, tiled=True),
        lax.psum_scatter(up_part, "mem", scatter_dimension=0, tiled=True),
    )
    activated = lax.all_gather(
        (jax.nn.silu(gate_sum) * up_sum).astype(jnp.bfloat16), "mem", axis=0, tiled=True
    )
    down_sum = lax.psum(
        jnp.dot(activated, down_weight, preferred_element_type=jnp.float32), ("head", "width")
    )
    return (middle_wide + down_sum).astype(jnp.bfloat16)


def solution(mesh):
    return jax.shard_map(
        per_device,
        mesh=mesh,
        in_specs=(
            P("groups", "mem"),
            P("mem"),
            P("mem", ("head", "width")),
            P("mem", ("head", "width")),
            P("mem", ("head", "width")),
            P(),
            P(),
            P(("groups", "mem"), ("head", "width"), None),
            P(("groups", "mem"), ("head", "width"), None),
            P(("groups", "mem")),
            P("groups"),
            P(("head", "width"), "mem"),
            P("mem"),
            P("mem", ("head", "width")),
            P("mem", ("head", "width")),
            P(("head", "width"), "mem"),
        ),
        out_specs=P("groups", "mem"),
        check_vma=False,
    )
```

profile of v0, /device:TPU:0, one launch (start us, length us, event | category | flops | bytes accessed | tf_op | source)
XLA Modules:
  0.0 318.0 jit_solution(10210930667824503828)
XLA Ops:
  7.7 13.5 %psum.49 = f32[32]{0:T(128)S(1)} all-reduce(f32[32]{0:T(128)S(1)} %fusion.24), channel_id=1, replica_groups=mesh['groups'=2,'mem'=4,'head'=2,'width'=2] {'mem'}, use_global_device_ids=true, to_apply=%region_2.0 | all-reduce | flops 32 | bytes 256 | tf_op jit(solution)/shard_map/psum | solution.py:79
  21.1 3.6 %convolution_bitcast_fusion.1 = f32[4,8,16,128]{3,1,2,0:T(8,128)S(1)} fusion(bf16[1280,2048]{1,0:T(8,128)(2,1)} %param.22, bf16[32,1280]{1,0:T(8,128)(2,1)} %param.20, f32[1280]{0:T(1024)} %param.21, f32[32]{0:T(128)S(1)} %add_rsqrt_fusion.3), kind=kOutput, calls=%fused_computation.38 | convolution fusion | flops 167936000 | bytes 5592192 | tf_op jit(solution)/shard_map/dot_general | solution.py:83
  27.3 32.1 %all-reduce.5.cloned.1.call-done = f32[32,16,128]{2,1,0:T(8,128)} async-done(((f32[32,16,128]{2,1,0:T(8,128)}), f32[32,16,128]{2,1,0:T(8,128)}) %all-reduce.5.cloned.1.call-update) | async-done | bytes 262160 | tf_op jit(solution)/shard_map/psum | solution.py:88
  62.2 12.0 %while.30 = (s32[]{:T(128)}, f32[32,2,8]{0,2,1:T(8,128)S(1)}, f32[32,2,8]{0,2,1:T(8,128)S(1)}, f32[32,2,8,128]{3,0,2,1:T(8,128)S(1)}, s32[]{:T(128)}, /*index=5*...) while((s32[]{:T(128)}, f32[32,2,8]{0,2,1:T(8,128)S(1)}, ...), condition=%wide.region_8.9_spmd.clone, body=%wide.region_5.8_spmd.clone.sunk | while | flops 274367744 | bytes 10269107 | solution.py:137
  62.3 2.0 constant_dynamic-slice_fusion.6
  66.3 1.9 constant_dynamic-slice_fusion.6
  70.3 1.9 constant_dynamic-slice_fusion.6
  75.5 39.0 %all-reduce = (bf16[32,256]{1,0:T(8,128)(2,1)S(1)}, f32[32,2,128]{2,0,1:T(8,128)S(1)}) all-reduce(f32[32,256]{1,0:T(8,128)S(1)} %fusion.45, f32[32,2,128]{2,0,1:T(8,128)S(1)} %bitcast.129), channel_id=1, replica_groups=mesh['groups'=2,'mem'=4,'head'=2,'width'=2] {'mem'}, use_global_device_ids=true, to_apply=%region_14.15 | all-reduce | flops 16384 | bytes 114688 | tf_op jit(solution)/shard_map/psum | solution.py:88
  114.9 14.1 %all-gather.1 = f32[128,2,8]{2,1,0:T(2,128)S(1)} all-gather(f32[32,2,8]{2,1,0:T(2,128)S(1)} %copy.92), channel_id=3, replica_groups=mesh['groups'=2,'mem'=4,'head'=2,'width'=2] {'mem'}, dimensions={0}, use_global_device_ids=true | all-gather | bytes 10240 | tf_op jit(solution)/shard_map/all_gather | solution.py:14
  129.0 13.3 %all-gather = f32[128,2,8]{2,1,0:T(2,128)S(1)} all-gather(f32[32,2,8]{2,1,0:T(2,128)S(1)} %copy.91), channel_id=2, replica_groups=mesh['groups'=2,'mem'=4,'head'=2,'width'=2] {'mem'}, dimensions={0}, use_global_device_ids=true | all-gather | bytes 10240 | tf_op jit(solution)/shard_map/all_gather | solution.py:14
  144.8 1.2 slice.53
  146.0 1.7 while.29
  148.8 4.1 %fusion.32 = f32[32,1280]{1,0:T(8,128)} fusion(bf16[2048,1280]{1,0:T(8,128)(2,1)} %param.31, bf16[4,8,16,128]{3,2,1,0:T(8,128)(2,1)S(1)} %bitcast.122), kind=kOutput, calls=%fused_computation.66 | convolution fusion | flops 167772160 | bytes 5537792 | tf_op jit(solution)/shard_map/dot_general | solution.py:168
  152.9 31.2 %all-reduce.7.cloned.1.call-done = f32[32,1280]{1,0:T(8,128)} async-done(((f32[32,1280]{1,0:T(8,128)}), f32[32,1280]{1,0:T(8,128)}) %all-reduce.7.cloned.1.call-update) | async-done | bytes 163856 | tf_op jit(solution)/shard_map/psum | solution.py:167
  185.1 11.7 %psum.54 = f32[32]{0:T(128)S(1)} all-reduce(f32[32]{0:T(128)S(1)} %get-tuple-element.230), channel_id=1, replica_groups=mesh['groups'=2,'mem'=4,'head'=2,'width'=2] {'mem'}, use_global_device_ids=true, to_apply=%region_18.19 | all-reduce | flops 32 | bytes 256 | tf_op jit(solution)/shard_map/psum | solution.py:172
  196.8 9.6 %fusion.37 = f32[32,6400]{1,0:T(8,128)} fusion(bf16[1280,6400]{1,0:T(8,128)(2,1)} %param.34, bf16[32,1280]{1,0:T(8,128)(2,1)S(1)} %get-tuple-element.231, f32[1280]{0:T(1024)S(1)} %copy-done.5, f32[32]{0:T(128)S(1)} %add_rsqrt_fusion.2), kind=kOutput, calls=%fused_computation.82 | convolution fusion | flops 524451840 | bytes 17290368 | tf_op jit(solution)/shard_map/dot_general | solution.py:177
  206.7 9.7 %fusion.39 = f32[32,6400]{1,0:T(8,128)} fusion(bf16[1280,6400]{1,0:T(8,128)(2,1)} %param.33, bf16[32,1280]{1,0:T(8,128)(2,1)S(1)} %get-tuple-element.231, f32[1280]{0:T(1024)S(1)} %copy-done.5, f32[32]{0:T(128)S(1)} %add_rsqrt_fusion.2), kind=kOutput, calls=%fused_computation.83 | convolution fusion | flops 524451840 | bytes 17290368 | tf_op jit(solution)/shard_map/dot_general | solution.py:176
  216.5 11.0 %reduce-scatter.5.cloned.1.call-done = f32[8,6400]{1,0:T(8,128)} async-done(((f32[32,6400]{1,0:T(8,128)}), f32[8,6400]{1,0:T(8,128)}) %reduce-scatter.5.cloned.1.call-update) | async-done | bytes 204816 | tf_op jit(solution)/shard_map/reduce_scatter | solution.py:180
  227.5 25.2 %reduce-scatter.3.cloned.1.call-done = f32[8,6400]{1,0:T(8,128)} async-done(((f32[32,6400]{1,0:T(8,128)}), f32[8,6400]{1,0:T(8,128)}) %reduce-scatter.3.cloned.1.call-update) | async-done | bytes 204816 | tf_op jit(solution)/shard_map/reduce_scatter | solution.py:179
  252.7 1.1 multiply_convert_fusion
  253.8 15.2 %all_gather.27 = bf16[32,6400]{1,0:T(8,128)(2,1)S(1)} all-gather(bf16[8,6400]{1,0:T(8,128)(2,1)S(1)} %multiply_convert_fusion), channel_id=1, replica_groups=mesh['groups'=2,'mem'=4,'head'=2,'width'=2] {'mem'}, dimensions={0}, use_global_device_ids=true | all-gather | bytes 512000 | tf_op jit(solution)/shard_map/all_gather | solution.py:182
  269.0 9.3 %fusion.52 = f32[32,1280]{1,0:T(8,128)} fusion(bf16[32,6400]{1,0:T(8,128)(2,1)S(1)} %all_gather.27, bf16[6400,1280]{1,0:T(8,128)(2,1)} %param.35), kind=kOutput, calls=%fused_computation.100 | convolution fusion | flops 524288000 | bytes 16957440 | tf_op jit(solution)/shard_map/dot_general | solution.py:186
  278.3 31.2 %all-reduce.9.cloned.1.call-done = f32[32,1280]{1,0:T(8,128)} async-done(((f32[32,1280]{1,0:T(8,128)}), f32[32,1280]{1,0:T(8,128)}) %all-reduce.9.cloned.1.call-update) | async-done | bytes 163856 | tf_op jit(solution)/shard_map/psum | solution.py:185
  309.5 1.6 fusion.31
  (132 shorter events, 19.6 us)
Async XLA Ops:
  6.5 68.4 %copy-start = (bf16[1280,256]{1,0:T(8,128)(2,1)S(1)}, bf16[1280,256]{1,0:T(8,128)(2,1)}, u32[]{:S(2)}) copy-start(bf16[1280,256]{1,0:T(8,128)(2,1)} %param.23) | copy-start | bytes 1966084
  6.5 19.0 %copy-start.6 = (s32[8192]{0:T(1024)S(1)}, s32[8192]{0:T(1024)}, u32[]{:S(2)}) copy-start(s32[8192]{0:T(1024)} %param.29) | copy-start | bytes 98308
  6.5 19.8 %copy-start.10 = (s32[16]{0:T(128)S(1)}, s32[16]{0:T(128)}, u32[]{:S(2)}) copy-start(s32[16]{0:T(128)} %param.30) | copy-start | bytes 196
  6.5 54.0 %copy-start.8 = (f32[128]{0:T(128)S(1)}, f32[128]{0:T(128)}, u32[]{:S(2)}) copy-start(f32[128]{0:T(128)} %param.25) | copy-start | bytes 1540
  6.5 52.9 %all-reduce.5.cloned.1.call-start = ((), (), s32[]{:S(2)}) async-start(), calls=%async_computation.2 | async-start | bytes 524288 | tf_op jit(solution)/shard_map/psum | solution.py:88
  25.5 118.1 %all-gather.5.cloned.1.call-start = ((), (), s32[]{:S(2)}) async-start(), calls=%async_computation.7 | async-start | bytes 1310720 | tf_op jit(solution)/shard_map/all_gather | solution.py:14
  62.1 12.8 %copy-start.2 = (bf16[32,1280]{1,0:T(8,128)(2,1)S(1)}, bf16[32,1280]{1,0:T(8,128)(2,1)}, u32[]{:S(2)}) copy-start(bf16[32,1280]{1,0:T(8,128)(2,1)} %param.20) | copy-start | bytes 245764
  62.1 12.8 %copy-start.7 = (f32[1280]{0:T(1024)S(1)}, f32[1280]{0:T(1024)}, u32[]{:S(2)}) copy-start(f32[1280]{0:T(1024)} %param.21) | copy-start | bytes 15364
  62.1 13.1 %copy-start.4 = (bf16[1280,256]{1,0:T(8,128)(2,1)S(1)}, bf16[1280,256]{1,0:T(8,128)(2,1)}, u32[]{:S(2)}) copy-start(bf16[1280,256]{1,0:T(8,128)(2,1)} %param.24) | copy-start | bytes 1966084
  62.2 52.4 %copy-start.9 = (f32[128]{0:T(128)S(1)}, f32[128]{0:T(128)}, u32[]{:S(2)}) copy-start(f32[128]{0:T(128)} %param.26) | copy-start | bytes 1540
  74.1 0.7 copy-start.3
  74.9 109.2 %all-reduce.7.cloned.1.call-start = ((), (), s32[]{:S(2)}) async-start(), calls=%async_computation.3 | async-start | bytes 327680 | tf_op jit(solution)/shard_map/psum | solution.py:167
  147.6 49.2 %copy-start.5 = (f32[1280]{0:T(1024)S(1)}, f32[1280]{0:T(1024)}, u32[]{:S(2)}) copy-start(f32[1280]{0:T(1024)} %param.32) | copy-start | bytes 15364
  152.9 74.6 %reduce-scatter.5.cloned.1.call-start = ((), (), s32[]{:S(2)}) async-start(), calls=%async_computation.5 | async-start | bytes 1024000 | tf_op jit(solution)/shard_map/reduce_scatter | solution.py:180
  206.4 46.3 %reduce-scatter.3.cloned.1.call-start = ((), (), s32[]{:S(2)}) async-start(), calls=%async_computation.4 | async-start | bytes 1024000 | tf_op jit(solution)/shard_map/reduce_scatter | solution.py:179
  216.4 93.1 %all-reduce.9.cloned.1.call-start = ((), (), s32[]{:S(2)}) async-start(), calls=%async_computation.6 | async-start | bytes 327680 | tf_op jit(solution)/shard_map/psum | solution.py:185
  269.0 42.1 %copy-start.1 = (bf16[1280,256]{1,0:T(8,128)(2,1)S(1)}, bf16[1280,256]{1,0:T(8,128)(2,1)}, u32[]{:S(2)}) copy-start(bf16[1280,256]{1,0:T(8,128)(2,1)} %param.23) | copy-start | bytes 1966084
Sparse Core Ops, SparseCore 0:
  25.6 33.7 all-reduce.4
  75.0 50.2 all-gather.4
  153.0 31.0 all-reduce.6
  206.6 20.8 reduce-scatter.4
  229.6 22.9 reduce-scatter.2
  278.4 31.0 all-reduce.8
where the time goes:
time: 319 us; the launch traced here: 318 us
  waiting for transfers between devices  131 us (41%)
  blocking collectives  107 us (34%)
  matrix products  41.5 us (13%)
  between operations  14.6 us (5%)
  other arithmetic  12 us (4%)
  local copies, waits for them, and re-layouts  11.5 us (4%)
    psum x1, blocking collectives, per_device(): lax.psum((query_part, key_part, value_part), 'mem')  39 us
    psum x1, waiting for transfers between devices, per_device(): lax.psum((query_part, key_part, value_part), 'mem')  32.1 us
    psum x1, waiting for transfers between devices, per_device(): lax.psum(jnp.dot(activated, down_weight, preferred_element_type=jnp.float...  31.2 us
    psum x1, waiting for transfers between devices, per_device(): lax.psum(jnp.dot(attended, output_weight, preferred_element_type=jnp.floa...  31.2 us
    all_gather x2, blocking collectives, combined_all(): pieces = jax.tree.map(lambda part: lax.all_gather(part, axis), value)  27.4 us
    reduce_scatter x1, waiting for transfers between devices, per_device(): lax.psum_scatter(gate_part, 'mem', scatter_dimension=0, tiled=True)  25.2 us
    all_gather x1, blocking collectives, per_device(): lax.all_gather((jax.nn.silu(gate_sum) * up_sum).astype(jnp.bfloat16), 'me...  15.2 us
    psum x1, blocking collectives, per_device(): squares = lax.psum(jnp.sum(residual * residual, axis=1), 'mem')  13.5 us
  transfers between devices with their start and end apart: 6, of which 5 were waited for; matrix products, arithmetic and copies ran while one was open for 4% of the time, Pallas kernels for 0%

commit v1 on v0

--- a/solution.py
+++ b/solution.py
@@ -182,8 +182,11 @@
     activated = lax.all_gather(
         (jax.nn.silu(gate_sum) * up_sum).astype(jnp.bfloat16), "mem", axis=0, tiled=True
     )
-    down_sum = lax.psum(
-        jnp.dot(activated, down_weight, preferred_element_type=jnp.float32), ("head", "width")
+    down_sum = jnp.sum(
+        lax.all_gather(
+            jnp.dot(activated, down_weight, preferred_element_type=jnp.float32), ("head", "width")
+        ),
+        axis=0,
     )
     return (middle_wide + down_sum).astype(jnp.bfloat16)
 

time: 319 us -> 293 us (0.918)
  waiting for transfers between devices: 131 us -> 99.6 us
  blocking collectives: 107 us -> 115 us
    psum x1 -> x0, waiting for transfers between devices: 31.2 us -> none  [per_device(): lax.psum(jnp.dot(activated, down_weight, preferred_element_type=jnp.float...]
    all_gather x0 -> x1, blocking collectives: none -> 7.85 us  [per_device(): lax.all_gather(jnp.dot(activated, down_weight, preferred_element_type=jnp...]
  transfers between devices with their start and end apart: 6 -> 5, of which waited for: 5 -> 4; matrix products, arithmetic and copies ran while one was open for 4% -> 4% of each run, Pallas kernels for 0% -> 0%
where the time goes in v1:
time: 293 us
  blocking collectives  115 us (39%)
  waiting for transfers between devices  99.6 us (34%)
  matrix products  40.8 us (14%)
  between operations  14.2 us (5%)
  local copies, waits for them, and re-layouts  11.5 us (4%)
  other arithmetic  11.2 us (4%)
    psum x1, blocking collectives, per_device(): lax.psum((query_part, key_part, value_part), 'mem')  39 us
    psum x1, waiting for transfers between devices, per_device(): lax.psum((query_part, key_part, value_part), 'mem')  32.1 us
    psum x1, waiting for transfers between devices, per_device(): lax.psum(jnp.dot(attended, output_weight, preferred_element_type=jnp.floa...  31.2 us
    all_gather x2, blocking collectives, combined_all(): pieces = jax.tree.map(lambda part: lax.all_gather(part, axis), value)  27.4 us
    reduce_scatter x1, waiting for transfers between devices, per_device(): lax.psum_scatter(gate_part, 'mem', scatter_dimension=0, tiled=True)  25.2 us
    all_gather x1, blocking collectives, per_device(): lax.all_gather((jax.nn.silu(gate_sum) * up_sum).astype(jnp.bfloat16), 'me...  15.2 us
    psum x1, blocking collectives, per_device(): squares = lax.psum(jnp.sum(residual * residual, axis=1), 'mem')  13.5 us
    psum x1, blocking collectives, per_device(): squares_mid = lax.psum(jnp.sum(middle_wide * middle_wide, axis=1), 'mem')  11.7 us
  transfers between devices with their start and end apart: 5, of which 4 were waited for; matrix products, arithmetic and copies ran while one was open for 4% of the time, Pallas kernels for 0%

profile of v1, /device:TPU:0, one launch (start us, length us, event | category | flops | bytes accessed | tf_op | source)
XLA Modules:
  0.0 292.7 jit_solution(11246626496092515100)
XLA Ops:
  7.7 13.5 %psum.42 = f32[32]{0:T(128)S(1)} all-reduce(f32[32]{0:T(128)S(1)} %fusion.24), channel_id=1, replica_groups=mesh['groups'=2,'mem'=4,'head'=2,'width'=2] {'mem'}, use_global_device_ids=true, to_apply=%region_2.0 | all-reduce | flops 32 | bytes 256 | tf_op jit(solution)/shard_map/psum | solution.py:79
  21.1 3.6 %convolution_bitcast_fusion.1 = f32[4,8,16,128]{3,1,2,0:T(8,128)S(1)} fusion(bf16[1280,2048]{1,0:T(8,128)(2,1)} %param.22, bf16[32,1280]{1,0:T(8,128)(2,1)} %param.20, f32[1280]{0:T(1024)} %param.21, f32[32]{0:T(128)S(1)} %add_rsqrt_fusion.3), kind=kOutput, calls=%fused_computation.38 | convolution fusion | flops 167936000 | bytes 5592192 | tf_op jit(solution)/shard_map/dot_general | solution.py:83
  27.3 32.1 %all-reduce.4.cloned.1.call-done = f32[32,16,128]{2,1,0:T(8,128)} async-done(((f32[32,16,128]{2,1,0:T(8,128)}), f32[32,16,128]{2,1,0:T(8,128)}) %all-reduce.4.cloned.1.call-update) | async-done | bytes 262160 | tf_op jit(solution)/shard_map/psum | solution.py:88
  59.5 1.1 multiply_reduce_fusion
  62.2 12.0 %while.30 = (s32[]{:T(128)}, f32[32,2,8]{0,2,1:T(8,128)S(1)}, f32[32,2,8]{0,2,1:T(8,128)S(1)}, f32[32,2,8,128]{3,0,2,1:T(8,128)S(1)}, s32[]{:T(128)}, /*index=5*...) while((s32[]{:T(128)}, f32[32,2,8]{0,2,1:T(8,128)S(1)}, ...), condition=%wide.region_8.9_spmd.clone, body=%wide.region_5.8_spmd.clone.sunk | while | flops 274367744 | bytes 10269107 | solution.py:137
  62.3 2.0 constant_dynamic-slice_fusion.6
  66.3 1.9 constant_dynamic-slice_fusion.6
  70.3 1.9 constant_dynamic-slice_fusion.6
  75.5 39.0 %all-reduce = (bf16[32,256]{1,0:T(8,128)(2,1)S(1)}, f32[32,2,128]{2,0,1:T(8,128)S(1)}) all-reduce(f32[32,256]{1,0:T(8,128)S(1)} %fusion.45, f32[32,2,128]{2,0,1:T(8,128)S(1)} %bitcast.131), channel_id=1, replica_groups=mesh['groups'=2,'mem'=4,'head'=2,'width'=2] {'mem'}, use_global_device_ids=true, to_apply=%region_14.15 | all-reduce | flops 16384 | bytes 114688 | tf_op jit(solution)/shard_map/psum | solution.py:88
  114.9 14.1 %all-gather.1 = f32[128,2,8]{2,1,0:T(2,128)S(1)} all-gather(f32[32,2,8]{2,1,0:T(2,128)S(1)} %copy.92), channel_id=3, replica_groups=mesh['groups'=2,'mem'=4,'head'=2,'width'=2] {'mem'}, dimensions={0}, use_global_device_ids=true | all-gather | bytes 10240 | tf_op jit(solution)/shard_map/all_gather | solution.py:14
  129.0 13.3 %all-gather = f32[128,2,8]{2,1,0:T(2,128)S(1)} all-gather(f32[32,2,8]{2,1,0:T(2,128)S(1)} %copy.91), channel_id=2, replica_groups=mesh['groups'=2,'mem'=4,'head'=2,'width'=2] {'mem'}, dimensions={0}, use_global_device_ids=true | all-gather | bytes 10240 | tf_op jit(solution)/shard_map/all_gather | solution.py:14
  144.8 1.2 slice.53
  146.0 1.7 while.29
  148.8 4.1 %fusion.32 = f32[32,1280]{1,0:T(8,128)} fusion(bf16[2048,1280]{1,0:T(8,128)(2,1)} %param.31, bf16[4,8,16,128]{3,2,1,0:T(8,128)(2,1)S(1)} %bitcast.124), kind=kOutput, calls=%fused_computation.66 | convolution fusion | flops 167772160 | bytes 5537792 | tf_op jit(solution)/shard_map/dot_general | solution.py:168
  152.9 31.2 %all-reduce.6.cloned.1.call-done = f32[32,1280]{1,0:T(8,128)} async-done(((f32[32,1280]{1,0:T(8,128)}), f32[32,1280]{1,0:T(8,128)}) %all-reduce.6.cloned.1.call-update) | async-done | bytes 163856 | tf_op jit(solution)/shard_map/psum | solution.py:167
  185.1 11.7 %psum.47 = f32[32]{0:T(128)S(1)} all-reduce(f32[32]{0:T(128)S(1)} %get-tuple-element.230), channel_id=1, replica_groups=mesh['groups'=2,'mem'=4,'head'=2,'width'=2] {'mem'}, use_global_device_ids=true, to_apply=%region_18.19 | all-reduce | flops 32 | bytes 256 | tf_op jit(solution)/shard_map/psum | solution.py:172
  196.8 9.6 %fusion.37 = f32[32,6400]{1,0:T(8,128)} fusion(bf16[1280,6400]{1,0:T(8,128)(2,1)} %param.34, bf16[32,1280]{1,0:T(8,128)(2,1)S(1)} %get-tuple-element.231, f32[1280]{0:T(1024)S(1)} %copy-done.5, f32[32]{0:T(128)S(1)} %add_rsqrt_fusion.2), kind=kOutput, calls=%fused_computation.82 | convolution fusion | flops 524451840 | bytes 17290368 | tf_op jit(solution)/shard_map/dot_general | solution.py:177
  206.7 9.7 %fusion.39 = f32[32,6400]{1,0:T(8,128)} fusion(bf16[1280,6400]{1,0:T(8,128)(2,1)} %param.33, bf16[32,1280]{1,0:T(8,128)(2,1)S(1)} %get-tuple-element.231, f32[1280]{0:T(1024)S(1)} %copy-done.5, f32[32]{0:T(128)S(1)} %add_rsqrt_fusion.2), kind=kOutput, calls=%fused_computation.83 | convolution fusion | flops 524451840 | bytes 17290368 | tf_op jit(solution)/shard_map/dot_general | solution.py:176
  216.4 11.1 %reduce-scatter.5.cloned.1.call-done = f32[8,6400]{1,0:T(8,128)} async-done(((f32[32,6400]{1,0:T(8,128)}), f32[8,6400]{1,0:T(8,128)}) %reduce-scatter.5.cloned.1.call-update) | async-done | bytes 204816 | tf_op jit(solution)/shard_map/reduce_scatter | solution.py:180
  227.5 25.2 %reduce-scatter.3.cloned.1.call-done = f32[8,6400]{1,0:T(8,128)} async-done(((f32[32,6400]{1,0:T(8,128)}), f32[8,6400]{1,0:T(8,128)}) %reduce-scatter.3.cloned.1.call-update) | async-done | bytes 204816 | tf_op jit(solution)/shard_map/reduce_scatter | solution.py:179
  252.7 1.1 multiply_convert_fusion
  253.8 15.2 %all_gather.33 = bf16[32,6400]{1,0:T(8,128)(2,1)S(1)} all-gather(bf16[8,6400]{1,0:T(8,128)(2,1)S(1)} %multiply_convert_fusion), channel_id=1, replica_groups=mesh['groups'=2,'mem'=4,'head'=2,'width'=2] {'mem'}, dimensions={0}, use_global_device_ids=true | all-gather | bytes 512000 | tf_op jit(solution)/shard_map/all_gather | solution.py:182
  269.0 8.6 %fusion.52 = f32[32,1280]{1,0:T(8,128)S(1)} fusion(bf16[32,6400]{1,0:T(8,128)(2,1)S(1)} %all_gather.33, bf16[6400,1280]{1,0:T(8,128)(2,1)} %param.35), kind=kOutput, calls=%fused_computation.100 | convolution fusion | flops 524288000 | bytes 16957440 | tf_op jit(solution)/shard_map/dot_general | solution.py:187
  277.6 7.9 %all-gather.3 = f32[128,1280]{1,0:T(8,128)S(1)} all-gather(f32[32,1280]{1,0:T(8,128)S(1)} %fusion.52), channel_id=5, replica_groups=mesh['groups'=2,'mem'=4,'head'=2,'width'=2] {'head','width'}, dimensions={0}, use_global_device_ids=true | all-gather | bytes 819200 | tf_op jit(solution)/shard_map/all_gather | solution.py:186
  (131 shorter events, 19.1 us)
Async XLA Ops:
  6.5 68.4 %copy-start = (bf16[1280,256]{1,0:T(8,128)(2,1)S(1)}, bf16[1280,256]{1,0:T(8,128)(2,1)}, u32[]{:S(2)}) copy-start(bf16[1280,256]{1,0:T(8,128)(2,1)} %param.23) | copy-start | bytes 1966084
  6.5 19.0 %copy-start.6 = (s32[8192]{0:T(1024)S(1)}, s32[8192]{0:T(1024)}, u32[]{:S(2)}) copy-start(s32[8192]{0:T(1024)} %param.29) | copy-start | bytes 98308
  6.5 19.8 %copy-start.10 = (s32[16]{0:T(128)S(1)}, s32[16]{0:T(128)}, u32[]{:S(2)}) copy-start(s32[16]{0:T(128)} %param.30) | copy-start | bytes 196
  6.5 54.0 %copy-start.8 = (f32[128]{0:T(128)S(1)}, f32[128]{0:T(128)}, u32[]{:S(2)}) copy-start(f32[128]{0:T(128)} %param.25) | copy-start | bytes 1540
  6.5 52.9 %all-reduce.4.cloned.1.call-start = ((), (), s32[]{:S(2)}) async-start(), calls=%async_computation.2 | async-start | bytes 524288 | tf_op jit(solution)/shard_map/psum | solution.py:88
  25.5 118.1 %all-gather.6.cloned.1.call-start = ((), (), s32[]{:S(2)}) async-start(), calls=%async_computation.6 | async-start | bytes 1310720 | tf_op jit(solution)/shard_map/all_gather | solution.py:14
  62.1 12.8 %copy-start.2 = (bf16[32,1280]{1,0:T(8,128)(2,1)S(1)}, bf16[32,1280]{1,0:T(8,128)(2,1)}, u32[]{:S(2)}) copy-start(bf16[32,1280]{1,0:T(8,128)(2,1)} %param.20) | copy-start | bytes 245764
  62.1 12.8 %copy-start.7 = (f32[1280]{0:T(1024)S(1)}, f32[1280]{0:T(1024)}, u32[]{:S(2)}) copy-start(f32[1280]{0:T(1024)} %param.21) | copy-start | bytes 15364
  62.1 13.1 %copy-start.4 = (bf16[1280,256]{1,0:T(8,128)(2,1)S(1)}, bf16[1280,256]{1,0:T(8,128)(2,1)}, u32[]{:S(2)}) copy-start(bf16[1280,256]{1,0:T(8,128)(2,1)} %param.24) | copy-start | bytes 1966084
  62.2 52.4 %copy-start.9 = (f32[128]{0:T(128)S(1)}, f32[128]{0:T(128)}, u32[]{:S(2)}) copy-start(f32[128]{0:T(128)} %param.26) | copy-start | bytes 1540
  74.1 0.7 copy-start.3
  74.9 109.2 %all-reduce.6.cloned.1.call-start = ((), (), s32[]{:S(2)}) async-start(), calls=%async_computation.3 | async-start | bytes 327680 | tf_op jit(solution)/shard_map/psum | solution.py:167
  147.6 49.2 %copy-start.5 = (f32[1280]{0:T(1024)S(1)}, f32[1280]{0:T(1024)}, u32[]{:S(2)}) copy-start(f32[1280]{0:T(1024)} %param.32) | copy-start | bytes 15364
  152.9 74.6 %reduce-scatter.5.cloned.1.call-start = ((), (), s32[]{:S(2)}) async-start(), calls=%async_computation.5 | async-start | bytes 1024000 | tf_op jit(solution)/shard_map/reduce_scatter | solution.py:180
  206.4 46.3 %reduce-scatter.3.cloned.1.call-start = ((), (), s32[]{:S(2)}) async-start(), calls=%async_computation.4 | async-start | bytes 1024000 | tf_op jit(solution)/shard_map/reduce_scatter | solution.py:179
  269.0 17.2 %copy-start.1 = (bf16[1280,256]{1,0:T(8,128)(2,1)S(1)}, bf16[1280,256]{1,0:T(8,128)(2,1)}, u32[]{:S(2)}) copy-start(bf16[1280,256]{1,0:T(8,128)(2,1)} %param.23) | copy-start | bytes 1966084
Sparse Core Ops, SparseCore 0:
  25.6 33.7 all-reduce.3
  75.0 50.2 all-gather.5
  153.0 31.0 all-reduce.5
  206.6 20.8 reduce-scatter.4
  229.6 22.9 reduce-scatter.2
